TPU v7x, 32 devices: a whole 2x2x4 slice. The times are simulated.
32 devices in a mesh: dp: 8 (over y, x, core), mp: 4 (over z).
Axes of the slice: x: 2, y: 2, z: 4, core: 2. Of those that a mesh axis runs over, the one named last changes fastest.
Arguments:
- pre: bfloat16 [1024, 12288], P('dp', 'mp'), may hold values from -32 to 32
- weight: float32 [6144, 12288], P('dp', 'mp'), may hold values from -0.0546875 to 0.0546875
- target: bfloat16 [6144, 1024], P('dp'), may hold values from -100 to 100
Outputs:
- update: float32 [6144, 12288], P('dp', 'mp')
All inputs are finite; a program needn't handle non-finite values.
Results may differ from a plain program's by a relative error of at most 0.0003.
The roundings to bfloat16 on the way count: a program that leaves them out, or rounds other values in their place, can miss the bound.
Values may be sent and summed in bfloat16 or wider, within the bound.
A program may use at most 64 MiB of HBM per device.

v0:
```python
import jax
import jax.numpy as jnp
from jax import lax
from jax.sharding import PartitionSpec as P

radius = 0.005
epsilon = 1e-06


def on_device(pre, weight, target):
    hidden = jax.nn.gelu(pre.astype(jnp.float32), approximate=False).astype(jnp.bfloat16)
    everyone = lax.all_gather(hidden, "dp", axis=0, tiled=True)
    entries = weight.shape[0] * weight.shape[1] * lax.axis_size("dp") * lax.axis_size("mp")

    def residual_of(matrix):
        partial_out = lax.dot_general(
            matrix, everyone, (((1,), (1,)), ((), ())), preferred_element_type=jnp.float32
        )
        summed = lax.psum(partial_out, "mp")
        result = (summed - target.astype(jnp.float32)).astype(jnp.bfloat16)
        return result

    resid = residual_of(weight.astype(jnp.bfloat16))
    ascent = jnp.dot(resid, everyone, preferred_element_type=jnp.float32)
    ascent_ms = lax.psum(jnp.sum(ascent * ascent), ("dp", "mp")) / entries
    perturbed = (weight + radius * jnp.tanh(ascent / jnp.sqrt(ascent_ms + epsilon))).astype(
        jnp.bfloat16
    )
    resid_two = residual_of(perturbed)
    descent = jnp.dot(resid_two, everyone, preferred_element_type=jnp.float32)
    descent_ms = lax.psum(jnp.sum(descent * descent), ("dp", "mp")) / entries
    return descent / jnp.sqrt(descent_ms + epsilon)


def solution(mesh):
    return jax.shard_map(
        on_device,
        mesh=mesh,
        in_specs=(P("dp", "mp"), P("dp", "mp"), P("dp", None)),
        out_specs=P("dp", "mp"),
        check_vma=False,
    )
```

profile of v0, /device:TPU:0, one launch (start us, length us, event | category | flops | bytes accessed | tf_op | source)
XLA Modules:
  0.0 443.9 jit_solution(3158897468256516652)
XLA Ops:
  6.5 0.0 all-gather.2.cloned.1.call-start
  6.5 5.1 %fusion.9 = bf16[128,3072]{1,0:T(8,128)(2,1)} fusion(bf16[128,3072]{1,0:T(8,128)(2,1)} %param.3), kind=kLoop, calls=%fused_computation.16 | loop fusion | flops 25952256 | bytes 1572864 | tf_op jit(solution)/shard_map/convert_element_type | solution.py:11
  11.7 0.0 all-gather.2.cloned.1.call-update
  11.7 0.0 all-reduce.3.cloned.1.call-start
  11.8 48.3 %all-gather.2.cloned.1.call-done = bf16[1024,3072]{1,0:T(8,128)(2,1)} async-done(((bf16[128,3072]{1,0:T(8,128)(2,1)}), bf16[1024,3072]{1,0:T(8,128)(2,1)}) %all-gather.2.cloned.1.call-update) | async-done | bytes 6291472 | tf_op jit(solution)/shard_map/all_gather | solution.py:12
  60.1 11.1 %fusion.5 = f32[768,1024]{1,0:T(8,128)} fusion(bf16[1024,3072]{1,0:T(8,128)(2,1)} %all-gather.2.cloned.1.call-done, f32[768,3072]{1,0:T(8,128)} %param.4), kind=kOutput, calls=%fused_computation.14 | convolution fusion | flops 4834197504 | bytes 18874368 | tf_op jit(solution)/shard_map/dot_general | solution.py:16
  71.2 0.0 copy-start
  71.2 0.0 all-reduce.3.cloned.1.call-update
  71.2 0.0 all-reduce.5.cloned.1.call-start
  71.2 121.2 %all-reduce.3.cloned.1.call-done = f32[768,1024]{1,0:T(8,128)} async-done(((f32[768,1024]{1,0:T(8,128)}), f32[768,1024]{1,0:T(8,128)}) %all-reduce.3.cloned.1.call-update) | async-done | bytes 3145744 | tf_op jit(solution)/shard_map/psum | solution.py:19
  192.4 0.0 copy-done
  192.4 11.1 %multiply_reduce_fusion.1 = (f32[]{:T(128)}, f32[768,3072]{1,0:T(8,128)}) fusion(bf16[1024,3072]{1,0:T(8,128)(2,1)} %all-gather.2.cloned.1.call-done, f32[768,1024]{1,0:T(8,128)} %all-reduce.3.cloned.1.call-done, bf16[768,1024]{1,0:T(8,128)(2,1)S(1)} %copy-done), kind=kOutput, calls=%fused_computation.2 | convolution fusion | flops 4838916096 | bytes 20447236 | tf_op jit(solution)/shard_map/dot_general | solution.py:24
  203.5 39.6 %psum.29 = f32[]{:T(128)} all-reduce(f32[]{:T(128)} %get-tuple-element.5), channel_id=1, replica_groups=mesh['dp'=8,'mp'=4] {'dp','mp'}, use_global_device_ids=true, to_apply=%region_2.0 | all-reduce | flops 1 | bytes 8 | tf_op jit(solution)/shard_map/psum | solution.py:25
  243.7 12.1 %fusion.2 = f32[768,1024]{1,0:T(8,128)} fusion(bf16[1024,3072]{1,0:T(8,128)(2,1)} %all-gather.2.cloned.1.call-done, f32[768,3072]{1,0:T(8,128)} %param.4, f32[768,3072]{1,0:T(8,128)} %get-tuple-element.6, f32[]{:T(128)S(6)} %sqrt.6), kind=kOutput, calls=%fused_computation.6 | convolution fusion | flops 4841275392 | bytes 28311556 | tf_op jit(solution)/shard_map/dot_general | solution.py:16
  255.8 0.0 all-reduce.5.cloned.1.call-update
  255.9 121.2 %all-reduce.5.cloned.1.call-done = f32[768,1024]{1,0:T(8,128)} async-done(((f32[768,1024]{1,0:T(8,128)}), f32[768,1024]{1,0:T(8,128)}) %all-reduce.5.cloned.1.call-update) | async-done | bytes 3145744 | tf_op jit(solution)/shard_map/psum | solution.py:19
  377.1 11.1 %multiply_reduce_fusion = (f32[]{:T(128)}, f32[768,3072]{1,0:T(8,128)}) fusion(bf16[1024,3072]{1,0:T(8,128)(2,1)} %all-gather.2.cloned.1.call-done, f32[768,1024]{1,0:T(8,128)} %all-reduce.5.cloned.1.call-done, bf16[768,1024]{1,0:T(8,128)(2,1)S(1)} %copy-done), kind=kOutput, calls=%fused_computation | convolution fusion | flops 4838916096 | bytes 20447236 | tf_op jit(solution)/shard_map/dot_general | solution.py:30
  388.2 39.4 %psum.31 = f32[]{:T(128)} all-reduce(f32[]{:T(128)} %get-tuple-element.7), channel_id=1, replica_groups=mesh['dp'=8,'mp'=4] {'dp','mp'}, use_global_device_ids=true, to_apply=%region_5.0 | all-reduce | flops 1 | bytes 8 | tf_op jit(solution)/shard_map/psum | solution.py:31
  428.3 9.0 %broadcast_divide_fusion = f32[768,3072]{1,0:T(8,128)} fusion(f32[768,3072]{1,0:T(8,128)} %get-tuple-element.8, f32[]{:T(128)S(6)} %sqrt.7), kind=kLoop, calls=%fused_computation.3 | loop fusion | flops 2359296 | bytes 18874372 | tf_op jit(solution)/shard_map/div | solution.py:32
Async XLA Ops:
  6.5 53.5 %all-gather.2.cloned.1.call-start = ((), (), s32[]{:S(2)}) async-start(), calls=%async_computation | async-start | bytes 7077888 | tf_op jit(solution)/shard_map/all_gather | solution.py:12
  11.7 180.7 %all-reduce.3.cloned.1.call-start = ((), (), s32[]{:S(2)}) async-start(), calls=%async_computation.1 | async-start | bytes 6291456 | tf_op jit(solution)/shard_map/psum | solution.py:19
  71.2 121.3 %copy-start = (bf16[768,1024]{1,0:T(8,128)(2,1)S(1)}, bf16[768,1024]{1,0:T(8,128)(2,1)}, u32[]{:S(2)}) copy-start(bf16[768,1024]{1,0:T(8,128)(2,1)} %param.5) | copy-start | bytes 4718596
  71.2 305.9 %all-reduce.5.cloned.1.call-start = ((), (), s32[]{:S(2)}) async-start(), calls=%async_computation.2 | async-start | bytes 6291456 | tf_op jit(solution)/shard_map/psum | solution.py:19
Sparse Core Ops, SparseCore 0:
  11.8 48.2 all-gather.1
  71.3 121.0 all-reduce.2
  256.0 121.0 all-reduce.4
where the time goes:
time: 444 us
  waiting for transfers between devices  291 us (66%)
  blocking collectives  79 us (18%)
  matrix products  45.4 us (10%)
  between operations  14.5 us (3%)
  other arithmetic  14.2 us (3%)
    psum x2, waiting for transfers between devices, residual_of(): summed = lax.psum(partial_out, 'mp')  242 us
    all_gather x1, waiting for transfers between devices, on_device(): everyone = lax.all_gather(hidden, 'dp', axis=0, tiled=True)  48.3 us
    psum x1, blocking collectives, on_device(): ascent_ms = lax.psum(jnp.sum(ascent * ascent), ('dp', 'mp')) / entries  39.6 us
    psum x1, blocking collectives, on_device(): descent_ms = lax.psum(jnp.sum(descent * descent), ('dp', 'mp')) / entries  39.4 us
    dot_general x2, matrix products, residual_of(): lax.dot_general(matrix, everyone, (((1,), (1,)), ((), ())), preferred_ele...  23.2 us
    dot_general x1, matrix products, on_device(): ascent = jnp.dot(resid, everyone, preferred_element_type=jnp.float32)  11.1 us
    dot_general x1, matrix products, on_device(): descent = jnp.dot(resid_two, everyone, preferred_element_type=jnp.float32)  11.1 us
    div x1, other arithmetic, on_device(): return descent / jnp.sqrt(descent_ms + epsilon)  9.05 us
  transfers between devices with their start and end apart: 3, of which 3 were waited for; matrix products, arithmetic and copies ran while one was open for 0% of the time, Pallas kernels for 0%

commit v1 on v0

--- a/solution.py
+++ b/solution.py
@@ -16,7 +16,12 @@
         partial_out = lax.dot_general(
             matrix, everyone, (((1,), (1,)), ((), ())), preferred_element_type=jnp.float32
         )
-        summed = lax.psum(partial_out, "mp")
+        parts_n = lax.axis_size("mp")
+        summed = partial_out
+        for at in [
+            [(ix, ix ^ pp) for ix in range(parts_n)] for pp in (1, 2, 4, 8, 16) if pp < parts_n
+        ]:
+            summed = summed + lax.ppermute(summed, "mp", at)
         result = (summed - target.astype(jnp.float32)).astype(jnp.bfloat16)
         return result
 

time: 444 us -> 614 us (1.38)
  waiting for transfers between devices: 291 us -> 452 us
  starting transfers between devices: 0.09 us -> 8.84 us
    ppermute x0 -> x4, waiting for transfers between devices: none -> 403 us  [residual_of(): summed = summed + lax.ppermute(summed, 'mp', at)]
    psum x2 -> x0, waiting for transfers between devices: 242 us -> none  [residual_of(): summed = lax.psum(partial_out, 'mp')]
    ppermute x0 -> x4, starting transfers between devices: none -> 8.84 us  [residual_of(): summed = summed + lax.ppermute(summed, 'mp', at)]
  transfers between devices with their start and end apart: 3 -> 5, of which waited for: 3 -> 5; matrix products, arithmetic and copies ran while one was open for 0% -> 0% of each run, Pallas kernels for 0% -> 0%
where the time goes in v1:
time: 614 us; the launch traced here: 613 us
  waiting for transfers between devices  452 us (74%)
  blocking collectives  77.1 us (13%)
  matrix products  43.3 us (7%)
  other arithmetic  15 us (2%)
  between operations  14.7 us (2%)
  starting transfers between devices  8.84 us (1%)
    ppermute x4, waiting for transfers between devices, residual_of(): summed = summed + lax.ppermute(summed, 'mp', at)  403 us
    all_gather x1, waiting for transfers between devices, on_device(): everyone = lax.all_gather(hidden, 'dp', axis=0, tiled=True)  48.4 us
    psum x1, blocking collectives, on_device(): ascent_ms = lax.psum(jnp.sum(ascent * ascent), ('dp', 'mp')) / entries  39 us
    psum x1, blocking collectives, on_device(): descent_ms = lax.psum(jnp.sum(descent * descent), ('dp', 'mp')) / entries  38.1 us
    dot_general x2, matrix products, residual_of(): lax.dot_general(matrix, everyone, (((1,), (1,)), ((), ())), preferred_ele...  21.1 us
    dot_general x1, matrix products, on_device(): ascent = jnp.dot(resid, everyone, preferred_element_type=jnp.float32)  13.1 us
  transfers between devices with their start and end apart: 5, of which 5 were waited for; matrix products, arithmetic and copies ran while one was open for 0% of the time, Pallas kernels for 0%

profile of v1, /device:TPU:0, one launch (start us, length us, event | category | flops | bytes accessed | tf_op | source)
XLA Modules:
  0.0 613.4 jit_solution(16383589734693682935)
XLA Ops:
  6.5 0.0 all-gather.2.cloned.1.call-start
  6.5 5.1 fusion.9
  11.7 0.0 all-gather.2.cloned.1.call-update
  11.7 48.4 %all-gather.2.cloned.1.call-done = bf16[1024,3072]{1,0:T(8,128)(2,1)} async-done(((bf16[128,3072]{1,0:T(8,128)(2,1)}), bf16[1024,3072]{1,0:T(8,128)(2,1)}) %all-gather.2.cloned.1.call-update) | async-done | bytes 6291472 | tf_op jit(solution)/shard_map/all_gather | solution.py:12
  60.1 9.5 %fusion.5 = f32[768,1024]{0,1:T(8,128)S(1)} fusion(bf16[1024,3072]{1,0:T(8,128)(2,1)} %all-gather.2.cloned.1.call-done, f32[768,3072]{1,0:T(8,128)} %param.4), kind=kOutput, calls=%fused_computation.14 | convolution fusion | flops 4834197504 | bytes 18874368 | tf_op jit(solution)/shard_map/dot_general | solution.py:16
  69.6 1.6 collective-permute-start
  71.2 68.8 %collective-permute-done = f32[768,1024]{0,1:T(8,128)S(1)} collective-permute-done((f32[768,1024]{0,1:T(8,128)S(1)}, f32[768,1024]{0,1:T(8,128)S(1)}, u32[]{:S(2)}, u32[]{:S(2)}) %collective-permute-start) | collective-permute-done | bytes 3145760 | tf_op jit(solution)/shard_map/ppermute | solution.py:24
  140.0 0.4 add.25
  140.4 2.5 collective-permute-start.1
  142.8 2.6 copy.4
  145.4 0.0 copy-done.1
  145.4 132.8 %collective-permute-done.1 = f32[768,1024]{0,1:T(8,128)} collective-permute-done((f32[768,1024]{0,1:T(8,128)S(1)}, f32[768,1024]{0,1:T(8,128)}, u32[]{:S(2)}, u32[]{:S(2)}) %collective-permute-start.1) | collective-permute-done | bytes 3145760 | tf_op jit(solution)/shard_map/ppermute | solution.py:24
  278.3 13.1 %multiply_reduce_fusion.1 = (f32[]{:T(128)}, f32[768,3072]{1,0:T(8,128)}) fusion(bf16[1024,3072]{1,0:T(8,128)(2,1)} %all-gather.2.cloned.1.call-done, bf16[768,1024]{0,1:T(8,128)(2,1)} %copy.4, f32[768,1024]{0,1:T(8,128)} %copy-done.1, f32[768,1024]{0,1:T(8,128)} %collective-permute-done.1), kind=kOutput, calls=%fused_computation.2 | convolution fusion | flops 4839702528 | bytes 23592964 | tf_op jit(solution)/shard_map/dot_general | solution.py:29
  291.4 39.0 %psum.14 = f32[]{:T(128)} all-reduce(f32[]{:T(128)} %get-tuple-element.5), channel_id=1, replica_groups=mesh['dp'=8,'mp'=4] {'dp','mp'}, use_global_device_ids=true, to_apply=%region_1.0 | all-reduce | flops 1 | bytes 8 | tf_op jit(solution)/shard_map/psum | solution.py:30
  331.0 0.0 slice-start.1
  331.0 11.6 %fusion.2 = f32[768,1024]{0,1:T(8,128)S(1)} fusion(bf16[1024,3072]{1,0:T(8,128)(2,1)} %all-gather.2.cloned.1.call-done, f32[768,3072]{1,0:T(8,128)} %param.4, f32[768,3072]{1,0:T(8,128)} %get-tuple-element.6, f32[]{:T(128)S(6)} %sqrt.6), kind=kOutput, calls=%fused_computation.6 | convolution fusion | flops 4841275392 | bytes 28311556 | tf_op jit(solution)/shard_map/dot_general | solution.py:16
  342.6 2.2 collective-permute-start.2
  344.8 67.5 %collective-permute-done.2 = f32[768,1024]{0,1:T(8,128)S(1)} collective-permute-done((f32[768,1024]{0,1:T(8,128)S(1)}, f32[768,1024]{0,1:T(8,128)S(1)}, u32[]{:S(2)}, u32[]{:S(2)}) %collective-permute-start.2) | collective-permute-done | bytes 3145760 | tf_op jit(solution)/shard_map/ppermute | solution.py:24
  412.3 0.4 add.29
  412.7 2.6 collective-permute-start.3
  415.3 134.3 %collective-permute-done.3 = f32[768,1024]{0,1:T(8,128)S(1)} collective-permute-done((f32[768,1024]{0,1:T(8,128)S(1)}, f32[768,1024]{0,1:T(8,128)S(1)}, u32[]{:S(2)}, u32[]{:S(2)}) %collective-permute-start.3) | collective-permute-done | bytes 3145760 | tf_op jit(solution)/shard_map/ppermute | solution.py:24
  549.7 9.1 %multiply_reduce_fusion = (f32[]{:T(128)}, f32[768,3072]{1,0:T(8,128)}) fusion(bf16[1024,3072]{1,0:T(8,128)(2,1)S(1)} %bitcast.7, bf16[768,1024]{0,1:T(8,128)(2,1)S(1)} %copy-done, f32[768,1024]{0,1:T(8,128)S(1)} %add.29, f32[768,1024]{0,1:T(8,128)S(1)} %collective-permute-done.3), kind=kOutput, calls=%fused_computation | convolution fusion | flops 4839702528 | bytes 23592964 | tf_op jit(solution)/shard_map/dot_general | solution.py:35
  558.7 38.1 %psum.15 = f32[]{:T(128)} all-reduce(f32[]{:T(128)} %get-tuple-element.7), channel_id=1, replica_groups=mesh['dp'=8,'mp'=4] {'dp','mp'}, use_global_device_ids=true, to_apply=%region_3.0 | all-reduce | flops 1 | bytes 8 | tf_op jit(solution)/shard_map/psum | solution.py:36
  597.5 9.0 %broadcast_divide_fusion = f32[768,3072]{1,0:T(8,128)} fusion(f32[768,3072]{1,0:T(8,128)} %get-tuple-element.8, f32[]{:T(128)S(6)} %sqrt.7), kind=kLoop, calls=%fused_computation.3 | loop fusion | flops 2359296 | bytes 18874372 | tf_op jit(solution)/shard_map/div | solution.py:37
  (7 shorter events, 0.0 us)
Async XLA Ops:
  6.5 53.5 %all-gather.2.cloned.1.call-start = ((), (), s32[]{:S(2)}) async-start(), calls=%async_computation | async-start | bytes 7077888 | tf_op jit(solution)/shard_map/all_gather | solution.py:12
  69.6 70.3 %collective-permute-start = (f32[768,1024]{0,1:T(8,128)S(1)}, f32[768,1024]{0,1:T(8,128)S(1)}, u32[]{:S(2)}, u32[]{:S(2)}) collective-permute-start(f32[768,1024]{0,1:T(8,128)S(1)} %fusion.5), channel_id=1, source_target_pairs={{0,1},{1,0},{2,3},{3,2},{4,5},{5,4},{6,7},{7,6},{8,9},{9,8},{10,11... | collective-permute-start | bytes 9437192 | tf_op jit(solution)/shard_map/ppermute | solution.py:24
  140.3 5.1 copy-start.1
  140.4 137.9 %collective-permute-start.1 = (f32[768,1024]{0,1:T(8,128)S(1)}, f32[768,1024]{0,1:T(8,128)}, u32[]{:S(2)}, u32[]{:S(2)}) collective-permute-start(f32[768,1024]{0,1:T(8,128)S(1)} %add.25), channel_id=1, source_target_pairs={{0,2},{1,3},{2,0},{3,1},{4,6},{5,7},{6,4},{7,5},{8,10},{9,11},{10,... | collective-permute-start | bytes 9437192 | tf_op jit(solution)/shard_map/ppermute | solution.py:24
  278.3 271.3 %slice-start = ((s8[6291456]{0:T(1024)(128)(4,1)}), s8[2097152]{0:T(1024)(128)(4,1)S(1)}, s32[]{:S(2)}) async-start(s8[6291456]{0:T(1024)(128)(4,1)} %bitcast.6), calls=%async_computation.1 | async-start | bytes 4194304
  331.0 218.7 %slice-start.1 = ((s8[6291456]{0:T(1024)(128)(4,1)}), s8[4194304]{0:T(1024)(128)(4,1)S(1)}, s32[]{:S(2)}) async-start(s8[6291456]{0:T(1024)(128)(4,1)} %bitcast.6), calls=%async_computation.2 | async-start | bytes 8388608
  342.6 207.0 %copy-start = (bf16[768,1024]{0,1:T(8,128)(2,1)S(1)}, bf16[768,1024]{0,1:T(8,128)(2,1)}, u32[]{:S(2)}) copy-start(bf16[768,1024]{0,1:T(8,128)(2,1)} %copy.4) | copy-start | bytes 4718596
  342.6 69.7 %collective-permute-start.2 = (f32[768,1024]{0,1:T(8,128)S(1)}, f32[768,1024]{0,1:T(8,128)S(1)}, u32[]{:S(2)}, u32[]{:S(2)}) collective-permute-start(f32[768,1024]{0,1:T(8,128)S(1)} %fusion.2), channel_id=1, source_target_pairs={{0,1},{1,0},{2,3},{3,2},{4,5},{5,4},{6,7},{7,6},{8,9},{9,8},{10,11... | collective-permute-start | bytes 9437192 | tf_op jit(solution)/shard_map/ppermute | solution.py:24
  412.7 136.9 %collective-permute-start.3 = (f32[768,1024]{0,1:T(8,128)S(1)}, f32[768,1024]{0,1:T(8,128)S(1)}, u32[]{:S(2)}, u32[]{:S(2)}) collective-permute-start(f32[768,1024]{0,1:T(8,128)S(1)} %add.29), channel_id=1, source_target_pairs={{0,2},{1,3},{2,0},{3,1},{4,6},{5,7},{6,4},{7,5},{8,10},{9,11},{10,... | collective-permute-start | bytes 9437192 | tf_op jit(solution)/shard_map/ppermute | solution.py:24
Sparse Core Ops, SparseCore 0:
  11.8 48.2 all-gather.1
